TPU v7x, 512 devices: a whole 4x4x16 slice. The times are simulated.
512 devices in a mesh: row: 32 (over z, x_lo), col: 16 (over x_hi, y, core).
Axes of the slice: x: 4 (x_hi: 2, x_lo: 2; x = x_hi * 2 + x_lo), y: 4, z: 16, core: 2. Of those that a mesh axis runs over, the one named last changes fastest.
Arguments:
- coupling: float32 [16384, 32, 512], P('col', 'row'), may hold values from -0.125 to 0.125
- lag_class: int32 [16, 32], P('col', 'row'), may hold values from 0 to 1
- rates_older: float32 [16, 32, 32, 2, 128], P('col', 'row'), may hold values from 0.05 to 0.95
- rates_newer: float32 [16, 32, 32, 2, 128], P('col', 'row'), may hold values from 0.05 to 0.95
- drive: float32 [3, 16, 32, 32, 2, 128], P(None, 'col', 'row'), may hold values from -6 to 6
- syn_kernel: float32 [128, 128], replicated, may hold values from 0 to 1, as said below
Outputs:
- rates: float32 [3, 16, 32, 32, 2, 128], P(None, 'col', 'row')
Inputs may be any that keep to these rules, and one draw needn't show every extreme that they name: syn_kernel is zero above its diagonal.
All inputs are finite; a program needn't handle non-finite values.
Results may differ from a plain program's by a relative error of at most 0.0001.
Values sent between devices are 32-bit elements; how exact they have to be, the bound alone decides.
A program may use at most 64 MiB of HBM per device.

v0:
```python
import jax
import jax.numpy as jnp
from jax import lax
from jax.sharding import PartitionSpec as P

PRECISE = lax.Precision.HIGHEST


def per_device(coupling, lag_class, rates_older, rates_newer, drive, syn_kernel):
    weights = coupling[:, 0, :]
    group = rates_newer.shape[2]
    runs = rates_newer.shape[3]
    steps = rates_newer.shape[4]
    width = runs * steps
    lag_near = lag_class[0, 0] == 0
    older_all, newer_all = (
        lax.all_gather(rates_older, "col", axis=0, tiled=True),
        lax.all_gather(rates_newer, "col", axis=0, tiled=True),
    )
    far_slab = older_all.reshape(-1, width)
    near_slab = newer_all.reshape(-1, width)
    produced = []
    for slab_index in range(drive.shape[0]):
        chosen = jnp.where(lag_near, near_slab, far_slab)
        partial_value = jnp.dot(
            weights, chosen, precision=PRECISE, preferred_element_type=jnp.float32
        )
        own_rows = lax.psum_scatter(partial_value, "row", scatter_dimension=0, tiled=True)
        filtered = jnp.dot(
            own_rows.reshape(group * runs, steps),
            syn_kernel.T,
            precision=PRECISE,
            preferred_element_type=jnp.float32,
        )
        fresh = jax.nn.sigmoid(filtered.reshape(group, runs, steps) + drive[slab_index, 0, 0])
        produced.append(fresh)
        if slab_index + 1 < drive.shape[0]:
            spread = lax.all_gather(fresh[None, None], "col", axis=0, tiled=True)
            far_slab, near_slab = (near_slab, spread.reshape(-1, width))
    return jnp.stack(produced)[:, None, None]


def solution(mesh):
    return jax.shard_map(
        per_device,
        mesh=mesh,
        in_specs=(
            P("col", "row", None),
            P("col", "row"),
            P("col", "row", None, None, None),
            P("col", "row", None, None, None),
            P(None, "col", "row", None, None, None),
            P(),
        ),
        out_specs=P(None, "col", "row", None, None, None),
        check_vma=False,
    )
```

profile of v0, /device:TPU:16, one launch (start us, length us, event | category | flops | bytes accessed | tf_op | source)
XLA Modules:
  0.0 539.6 jit_solution(9030777055588399325)
XLA Ops:
  7.3 0.8 copy.30
  8.1 0.8 copy.29
  8.9 21.1 %all_gather.12 = f32[16,1,32,2,128]{4,2,3,1,0:T(8,128)S(1)} all-gather(f32[1,1,32,2,128]{4,2,3,1,0:T(8,128)S(1)} %copy.29), channel_id=1, replica_groups=mesh['row'=32,'col'=16] {'col'}, dimensions={0}, use_global_device_ids=true | all-gather | bytes 557056 | tf_op jit(solution)/shard_map/all_gather | solution.py:18
  30.0 22.2 %all_gather.13 = f32[16,1,32,2,128]{4,2,3,1,0:T(8,128)S(1)} all-gather(f32[1,1,32,2,128]{4,2,3,1,0:T(8,128)S(1)} %copy.30), channel_id=1, replica_groups=mesh['row'=32,'col'=16] {'col'}, dimensions={0}, use_global_device_ids=true | all-gather | bytes 557056 | tf_op jit(solution)/shard_map/all_gather | solution.py:17
  52.2 0.1 broadcast_select_fusion
  52.3 0.4 copy.31
  52.7 4.5 fusion.9
  57.2 2.6 copy.47
  59.8 0.0 reduce-scatter.12.cloned.1.call-start
  59.9 142.0 %reduce-scatter.10.cloned.1.call-done = f32[32,256]{1,0:T(8,128)} async-done(((f32[1024,256]{1,0:T(8,128)}), f32[32,256]{1,0:T(8,128)}) %reduce-scatter.10.cloned.1.call-update) | async-done | bytes 32784
  201.9 0.9 copy.48
  202.7 0.4 fusion.30
  203.1 20.8 %all-gather = f32[512,2,128]{2,0,1:T(8,128)S(1)} all-gather(f32[32,2,128]{2,0,1:T(8,128)S(1)} %fusion.30), channel_id=2, replica_groups=mesh['row'=32,'col'=16] {'col'}, dimensions={0}, use_global_device_ids=true | all-gather | bytes 557056 | tf_op jit(solution)/shard_map/all_gather | solution.py:38
  223.9 0.1 copy_select_fusion.1
  224.0 0.4 copy.35
  224.4 4.5 fusion.12
  229.0 2.5 copy.49
  231.5 0.0 reduce-scatter.12.cloned.1.call-update
  231.5 0.0 reduce-scatter.14.cloned.1.call-start
  231.6 136.0 %reduce-scatter.12.cloned.1.call-done = f32[32,256]{1,0:T(8,128)} async-done(((f32[1024,256]{1,0:T(8,128)}), f32[32,256]{1,0:T(8,128)}) %reduce-scatter.12.cloned.1.call-update) | async-done | bytes 32784
  367.5 0.9 copy.50
  368.4 0.4 fusion.26
  368.8 21.0 %all-gather.1 = f32[512,2,128]{2,0,1:T(8,128)S(1)} all-gather(f32[32,2,128]{2,0,1:T(8,128)S(1)} %fusion.26), channel_id=3, replica_groups=mesh['row'=32,'col'=16] {'col'}, dimensions={0}, use_global_device_ids=true | all-gather | bytes 557056 | tf_op jit(solution)/shard_map/all_gather | solution.py:38
  389.7 0.1 copy_select_fusion
  389.8 0.4 copy.40
  390.2 3.5 fusion.15
  393.7 1.3 copy.51
  395.0 0.0 reduce-scatter.14.cloned.1.call-update
  395.1 136.0 %reduce-scatter.14.cloned.1.call-done = f32[32,256]{1,0:T(8,128)} async-done(((f32[1024,256]{1,0:T(8,128)}), f32[32,256]{1,0:T(8,128)}) %reduce-scatter.14.cloned.1.call-update) | async-done | bytes 32784
  531.1 0.9 copy.52
  531.9 0.4 fusion.22
  532.3 0.7 copy.43
  (10 shorter events, 0.0 us)
Async XLA Ops:
  6.5 196.2 %copy-start = (f32[128,128]{1,0:T(8,128)S(1)}, f32[128,128]{1,0:T(8,128)}, u32[]{:S(2)}) copy-start(f32[128,128]{1,0:T(8,128)} %param.11) | copy-start | bytes 196612
  6.5 46.1 %copy-start.1 = (f32[1024,1,512]{2,1,0:T(1,128)S(1)}, f32[1024,1,512]{2,1,0:T(1,128)}, u32[]{:S(2)}) copy-start(f32[1024,1,512]{2,1,0:T(1,128)} %param.6) | copy-start | bytes 6291460
  6.5 195.3 %reduce-scatter.10.cloned.1.call-start = ((), (), s32[]{:S(2)}) async-start(), calls=%async_computation.3 | async-start | bytes 1081344
  57.2 2.6 copy-start.2
  59.8 307.7 %reduce-scatter.12.cloned.1.call-start = ((), (), s32[]{:S(2)}) async-start(), calls=%async_computation.4 | async-start | bytes 1081344
  231.5 299.6 %reduce-scatter.14.cloned.1.call-start = ((), (), s32[]{:S(2)}) async-start(), calls=%async_computation.5 | async-start | bytes 1081344
Sparse Core Ops, SparseCore 0:
  59.9 141.9 reduce-scatter.9
  231.6 135.8 reduce-scatter.11
  395.2 135.8 reduce-scatter.13
where the time goes:
time: 540 us
  waiting for transfers between devices  414 us (77%)
  blocking collectives  85.1 us (16%)
  between operations  14 us (3%)
  matrix products  13.7 us (3%)
  local copies, waits for them, and re-layouts  12.4 us (2%)
    unnamed x6, waiting for transfers between devices  414 us
    all_gather x2, blocking collectives, per_device(): spread = lax.all_gather(fresh[None, None], 'col', axis=0, tiled=True)  41.8 us
    all_gather x1, blocking collectives, per_device(): lax.all_gather(rates_older, 'col', axis=0, tiled=True)  22.2 us
    all_gather x1, blocking collectives, per_device(): lax.all_gather(rates_newer, 'col', axis=0, tiled=True)  21.1 us
    dot_general x3, matrix products, per_device(): jnp.dot(weights, chosen, precision=PRECISE, preferred_element_type=jnp.fl...  12.6 us
  transfers between devices with their start and end apart: 3, of which 3 were waited for; matrix products, arithmetic and copies ran while one was open for 0% of the time, Pallas kernels for 0%

commit v1 on v0

v1 whole, which is shorter than its diff:
```python
import functools

import jax
import jax.numpy as jnp
from jax import lax
from jax.experimental import pallas as pl
from jax.experimental.pallas import tpu as pltpu
from jax.sharding import PartitionSpec as P

MESH = pl.DeviceIdType.MESH
N_Z = 16
ROWS = 32
LANES = 128
SLABS = 3
RUNS = 2
LAG = 3

OFFSETS = (8, 7, -7, 6, 5, -6, -5, 4, 3, -4, -3, 2, 1, -2, -1, 0)
PLACE = {offset: place for place, offset in enumerate(OFFSETS)}
PLACE[-8] = PLACE[8]
GROUPS = ((0, 3), (3, 7), (7, 11), (11, 15), (15, 16))


def kernel(
    coupling, lag_class, older, newer, drive, syn_kernel, out,
    w_raw, w_hi, w_lo, seen, rhs, own, x_send, x_recv, z_send, z_recv, z_last,
    older_v, newer_v, drive_v, syn_v, kt_hi, kt_lo,
    load_sem, w_sem, gather_sem, x_sem, z_sem, last_sem, send_sem, first_send_sem,
):
    row, col = lax.axis_index("row"), lax.axis_index("col")
    z, x_lo = row // 2, row % 2
    x_hi, y, core = col // 8, (col // 2) % 4, col % 2

    loads = [
        pltpu.make_async_copy(src, dst, load_sem.at[i])
        for i, (src, dst) in enumerate(
            ((older, older_v), (newer, newer_v), (drive, drive_v), (syn_kernel, syn_v))
        )
    ]
    for load in loads:
        load.start()

    def z_device(step):
        return (lax.rem(z + step + N_Z, N_Z) * 2 + x_lo, col)

    x_device = (z * 2 + 1 - x_lo, col)
    peers = []
    for dx in (1, 0):
        for dy in (2, 1, 3, 0):
            for dc in (1, 0):
                if (dx, dy, dc) != (0, 0, 0):
                    other = (
                        lax.rem(x_hi + dx, 2) * 8
                        + lax.rem(y + dy, 4) * 2
                        + lax.rem(core + dc, 2)
                    )
                    peers.append((row, other))

    barrier = pltpu.get_barrier_semaphore()
    partners = peers + [x_device] + [z_device(s) for s in (1, -1, 2, -2)]
    for device in partners:
        pl.semaphore_signal(barrier, inc=1, device_id=device, device_id_type=MESH)

    w_loads = []
    for half in range(2):
        for place, offset in enumerate(OFFSETS):
            x_of = 1 - x_lo if half == 0 else x_lo
            block = lax.rem(z + offset + N_Z, N_Z) * 2 + x_of
            at = half * 16 + place
            w_loads.append(
                pltpu.make_async_copy(
                    coupling.at[pl.ds(pl.multiple_of(block * 128, 128), 128)],
                    w_raw.at[pl.ds(at * 128, 128)],
                    w_sem.at[at],
                )
            )
    for load in w_loads:
        load.start()

    mine = pl.multiple_of(col * ROWS, ROWS)

    def send_all(slab, run, sem, recv):
        block = seen.at[slab, run, pl.ds(mine, ROWS)]
        for device in peers:
            pltpu.make_async_remote_copy(
                src_ref=block, dst_ref=block, send_sem=sem, recv_sem=recv,
                device_id=device, device_id_type=MESH,
            ).start()

    loads[0].wait()
    loads[1].wait()
    for run in range(RUNS):
        seen[0, run, pl.ds(mine, ROWS), :] = older_v[pl.ds(run, ROWS, stride=2), :]
        seen[1, run, pl.ds(mine, ROWS), :] = newer_v[pl.ds(run, ROWS, stride=2), :]
    pl.semaphore_wait(barrier, len(partners))
    for run in range(RUNS):
        for slab in range(2):
            send_all(slab, run, first_send_sem.at[slab, run], gather_sem.at[slab, run])

    loads[2].wait()
    loads[3].wait()
    kt = syn_v[...].T
    kt_h = kt.astype(jnp.bfloat16)
    kt_hi[...] = kt_h
    kt_lo[...] = (kt - kt_h.astype(jnp.float32)).astype(jnp.bfloat16)

    for load in w_loads:
        load.wait()

    def split(at, carry):
        rows = pl.ds(pl.multiple_of(at * ROWS, ROWS), ROWS)
        for q in range(4):
            w = w_raw[pl.ds(at * 128 + q, ROWS, stride=4), :]
            w_h = w.astype(jnp.bfloat16)
            w_hi[rows, q * LANES : (q + 1) * LANES] = w_h
            w_lo[rows, q * LANES : (q + 1) * LANES] = (
                w - w_h.astype(jnp.float32)
            ).astype(jnp.bfloat16)
        return carry

    lax.fori_loop(0, 32, split, 0)

    def gather_wait(slab, run):
        rest = seen.at[slab, run, pl.ds(0, 15 * ROWS)]
        pltpu.make_async_copy(rest, rest, gather_sem.at[slab, run]).wait()

    def product(run, first, count):
        rows = pl.ds(first * ROWS, count * ROWS)
        both = jnp.dot(w_hi[rows, :], rhs[run], preferred_element_type=jnp.float32)
        low = jnp.dot(
            w_lo[rows, :], rhs[run, :, :LANES], preferred_element_type=jnp.float32
        )
        return both[:, :LANES] + (both[:, LANES:] + low)

    def x_copy(slab, run, group):
        first, last = GROUPS[group]
        rows = pl.ds(first * ROWS, (last - first) * ROWS)
        return pltpu.make_async_remote_copy(
            src_ref=x_send.at[slab, run, rows],
            dst_ref=x_recv.at[slab, run, rows],
            send_sem=send_sem.at[slab, run],
            recv_sem=x_sem.at[slab, run, group],
            device_id=x_device, device_id_type=MESH,
        )

    def multiply(slab, run):
        if slab == 0:
            gather_wait(0, run)
        gather_wait(slab + 1, run)
        lag = jnp.broadcast_to(lag_class[0, 0], (16 * ROWS, LANES))
        chosen = jnp.where(lag == 0, seen[slab + 1, run], seen[slab, run])
        high = chosen.astype(jnp.bfloat16)
        rhs[run, :, :LANES] = high
        rhs[run, :, LANES:] = (chosen - high.astype(jnp.float32)).astype(jnp.bfloat16)
        for group, (first, last) in enumerate(GROUPS):
            x_send[slab, run, first * ROWS : last * ROWS, :] = product(run, first, last - first)
            x_copy(slab, run, group).start()
        for first, last in GROUPS:
            own[slab, run, first * ROWS : last * ROWS, :] = product(
                run, 16 + first, last - first
            )

    def pair_offsets(way, run, step):
        sign = 1 if way == 0 else -1
        far, near = sign * (8 - 2 * step), sign * (7 - 2 * step)
        return (None if step == 0 and way != run else far), near

    def z_copy(slab, run, way, step):
        far, _ = pair_offsets(way, run, step)
        first = 0 if far is not None else ROWS
        rows = pl.ds(step * 2 * ROWS + first, 2 * ROWS - first)
        return pltpu.make_async_remote_copy(
            src_ref=z_send.at[slab, run, way, rows],
            dst_ref=z_recv.at[slab, run, way, rows],
            send_sem=send_sem.at[slab, run],
            recv_sem=z_sem.at[slab, run, way, step],
            device_id=z_device(2 if way == 0 else -2), device_id_type=MESH,
        )

    def last_copy(slab, run, way, which):
        sign = 1 if way == 0 else -1
        return pltpu.make_async_remote_copy(
            src_ref=z_send.at[slab, run, way, pl.ds((6 + which) * ROWS, ROWS)],
            dst_ref=z_last.at[slab, run, pl.ds((2 * way + which) * ROWS, ROWS)],
            send_sem=send_sem.at[slab, run],
            recv_sem=last_sem.at[slab, run, way, which],
            device_id=z_device(sign * (2 - which)), device_id_type=MESH,
        )

    def pass_on(slab, run, step):
        x_copy(slab, run, step).wait_recv()
        for way in range(2):
            if step:
                z_copy(slab, run, way, step - 1).wait_recv()
            for which, offset in enumerate(pair_offsets(way, run, step)):
                if offset is None:
                    continue
                at = PLACE[offset] * ROWS
                total = (
                    own[slab, run, at : at + ROWS, :] + x_recv[slab, run, at : at + ROWS, :]
                )
                if step and pair_offsets(way, run, step - 1)[which] is not None:
                    came = ((step - 1) * 2 + which) * ROWS
                    total = total + z_recv[slab, run, way, came : came + ROWS, :]
                to = (step * 2 + which) * ROWS
                z_send[slab, run, way, to : to + ROWS, :] = total
            if step < 3:
                z_copy(slab, run, way, step).start()
            else:
                for which in range(2):
                    last_copy(slab, run, way, which).start()

    def finish(slab, run):
        x_copy(slab, run, 4).wait_recv()
        total = own[slab, run, 15 * ROWS :, :] + x_recv[slab, run, 15 * ROWS :, :]
        for which in (1, 0):
            for way in range(2):
                last_copy(slab, run, way, which).wait_recv()
                came = (2 * way + which) * ROWS
                total = total + z_last[slab, run, came : came + ROWS, :]
        high = total.astype(jnp.bfloat16)
        low = (total - high.astype(jnp.float32)).astype(jnp.bfloat16)
        filtered = jnp.dot(high, kt_hi[...], preferred_element_type=jnp.float32) + (
            jnp.dot(high, kt_lo[...], preferred_element_type=jnp.float32)
            + jnp.dot(low, kt_hi[...], preferred_element_type=jnp.float32)
        )
        value = filtered + drive_v[slab, pl.ds(run, ROWS, stride=2), :]
        fresh = 1.0 / (1.0 + jnp.exp(-value))
        if slab < SLABS - 1:
            seen[slab + 2, run, pl.ds(mine, ROWS), :] = fresh
            send_all(slab + 2, run, send_sem.at[slab, run], gather_sem.at[slab + 2, run])
        out[slab, pl.ds(run, ROWS, stride=2), :] = fresh

    stages = []
    for run in range(RUNS):
        line = []
        for slab in range(SLABS):
            line.append(functools.partial(multiply, slab, run))
            for step in range(4):
                line.append(functools.partial(pass_on, slab, run, step))
            line.append(functools.partial(finish, slab, run))
        stages.append(line)
    for at in range(len(stages[0]) + LAG):
        for run in range(RUNS):
            if 0 <= at - LAG * run < len(stages[run]):
                stages[run][at - LAG * run]()

    for run in range(RUNS):
        for slab in range(2):
            rest = seen.at[slab, run, pl.ds(0, 15 * ROWS)]
            pltpu.make_async_copy(rest, rest, first_send_sem.at[slab, run]).wait()
        for slab in range(SLABS):
            blocks = 16 + 15 + (15 if slab < SLABS - 1 else 0)
            sent = w_raw.at[pl.ds(0, blocks * ROWS)]
            pltpu.make_async_copy(sent, sent, send_sem.at[slab, run]).wait()


def per_device(coupling, lag_class, rates_older, rates_newer, drive, syn_kernel):
    f32, bf16 = jnp.float32, jnp.bfloat16
    rates = pl.pallas_call(
        kernel,
        out_shape=jax.ShapeDtypeStruct((SLABS, 64, LANES), f32),
        in_specs=[
            pl.BlockSpec(memory_space=pl.ANY),
            pl.BlockSpec(memory_space=pltpu.SMEM),
            pl.BlockSpec(memory_space=pl.ANY),
            pl.BlockSpec(memory_space=pl.ANY),
            pl.BlockSpec(memory_space=pl.ANY),
            pl.BlockSpec(memory_space=pl.ANY),
        ],
        out_specs=pl.BlockSpec(memory_space=pltpu.VMEM),
        scratch_shapes=[
            pltpu.VMEM((4096, LANES), f32),
            pltpu.VMEM((1024, 512), bf16),
            pltpu.VMEM((1024, 512), bf16),
            pltpu.VMEM((4, RUNS, 512, LANES), f32),
            pltpu.VMEM((RUNS, 512, 2 * LANES), bf16),
            pltpu.VMEM((SLABS, RUNS, 512, LANES), f32),
            pltpu.VMEM((SLABS, RUNS, 512, LANES), f32),
            pltpu.VMEM((SLABS, RUNS, 512, LANES), f32),
            pltpu.VMEM((SLABS, RUNS, 2, 8 * ROWS, LANES), f32),
            pltpu.VMEM((SLABS, RUNS, 2, 8 * ROWS, LANES), f32),
            pltpu.VMEM((SLABS, RUNS, 4 * ROWS, LANES), f32),
            pltpu.VMEM((64, LANES), f32),
            pltpu.VMEM((64, LANES), f32),
            pltpu.VMEM((SLABS, 64, LANES), f32),
            pltpu.VMEM((LANES, LANES), f32),
            pltpu.VMEM((LANES, LANES), bf16),
            pltpu.VMEM((LANES, LANES), bf16),
            pltpu.SemaphoreType.DMA((4,)),
            pltpu.SemaphoreType.DMA((32,)),
            pltpu.SemaphoreType.DMA((4, RUNS)),
            pltpu.SemaphoreType.DMA((SLABS, RUNS, 5)),
            pltpu.SemaphoreType.DMA((SLABS, RUNS, 2, 3)),
            pltpu.SemaphoreType.DMA((SLABS, RUNS, 2, 2)),
            pltpu.SemaphoreType.DMA((SLABS, RUNS)),
            pltpu.SemaphoreType.DMA((2, RUNS)),
        ],
        compiler_params=pltpu.CompilerParams(collective_id=0, has_side_effects=True),
    )(
        coupling.reshape(4096, LANES),
        lag_class,
        rates_older.reshape(64, LANES),
        rates_newer.reshape(64, LANES),
        drive.reshape(SLABS, 64, LANES),
        syn_kernel,
    )
    return rates.reshape(drive.shape)


def solution(mesh):
    return jax.shard_map(
        per_device,
        mesh=mesh,
        in_specs=(
            P("col", "row", None),
            P("col", "row"),
            P("col", "row", None, None, None),
            P("col", "row", None, None, None),
            P(None, "col", "row", None, None, None),
            P(),
        ),
        out_specs=P(None, "col", "row", None, None, None),
        check_vma=False,
    )
```

time: 540 us -> 117 us (0.22)
  the two profiles are of different devices: /device:TPU:16 before, /device:TPU:64 now
where the time goes in v1:
time: 117 us
  Pallas kernels  115 us (98%)
  local copies, waits for them, and re-layouts  1.54 us (1%)
    pallas_call x1, Pallas kernels, per_device(): pl.pallas_call(kernel, out_shape=jax.ShapeDtypeStruct((SLABS, 64, LANES),...  115 us

profile of v1, /device:TPU:64, one launch (start us, length us, event | category | flops | bytes accessed | tf_op | source)
XLA Modules:
  0.0 116.8 jit_solution(6395325700124854888)
XLA Ops:
  0.7 114.6 %shard_map.64 = f32[3,64,128]{2,1,0:T(8,128)} custom-call(f32[4096,128]{1,0:T(8,128)} %bitcast.7, s32[1,1]{1,0:T(1,128)S(6)} %copy.9.lag_class, f32[64,128]{1,0:T(8,128)} %bitcast.10, f32[64,128]{1,0:T(8,128)} %bitcast.11, f32[3,64,128]{2,1,0:T(8,128)} %bitcast.9, f32[128,128]{1,0:T(8,128)} %syn_kernel.1), custom_call_target="tpu_custom_call" | custom-call | tf_op jit(solution)/shard_map/pallas_call | solution.py:260
  115.3 1.5 %copy.10 = f32[3,1,1,32,2,128]{5,4,3,2,1,0:T(2,128)} copy(f32[3,1,1,32,2,128]{5,4,3,2,1,0:T(2,128)} %bitcast.8) | data formatting | bytes 196608

commit v2 on v1

--- a/solution.py
+++ b/solution.py
@@ -13,19 +13,21 @@
 LANES = 128
 SLABS = 3
 RUNS = 2
-LAG = 3
+LAG = 1
+PIECE = 32
 
 OFFSETS = (8, 7, -7, 6, 5, -6, -5, 4, 3, -4, -3, 2, 1, -2, -1, 0)
 PLACE = {offset: place for place, offset in enumerate(OFFSETS)}
 PLACE[-8] = PLACE[8]
+PIECES = ROWS // PIECE
 GROUPS = ((0, 3), (3, 7), (7, 11), (11, 15), (15, 16))
 
 
 def kernel(
     coupling, lag_class, older, newer, drive, syn_kernel, out,
-    w_raw, w_hi, w_lo, seen, rhs, own, x_send, x_recv, z_send, z_recv, z_last,
+    w_raw, w_hi, w_lo, seen, rhs, own, x_send, x_recv, z_send, z_recv,
     older_v, newer_v, drive_v, syn_v, kt_hi, kt_lo,
-    load_sem, w_sem, gather_sem, x_sem, z_sem, last_sem, send_sem, first_send_sem,
+    load_sem, w_sem, gather_sem, relay_sem, x_sem, z_sem, send_sem, first_send_sem,
 ):
     row, col = lax.axis_index("row"), lax.axis_index("col")
     z, x_lo = row // 2, row % 2
@@ -44,20 +46,14 @@
         return (lax.rem(z + step + N_Z, N_Z) * 2 + x_lo, col)
 
     x_device = (z * 2 + 1 - x_lo, col)
-    peers = []
-    for dx in (1, 0):
-        for dy in (2, 1, 3, 0):
-            for dc in (1, 0):
-                if (dx, dy, dc) != (0, 0, 0):
-                    other = (
-                        lax.rem(x_hi + dx, 2) * 8
-                        + lax.rem(y + dy, 4) * 2
-                        + lax.rem(core + dc, 2)
-                    )
-                    peers.append((row, other))
+    peers = [
+        (row, lax.rem(x_hi + dx, 2) * 8 + lax.rem(y + dy, 4) * 2 + core)
+        for dx, dy in ((1, 2), (1, 1), (1, 3), (1, 0), (0, 2), (0, 1), (0, 3))
+    ]
+    sibling = (row, col + 1 - 2 * core)
 
     barrier = pltpu.get_barrier_semaphore()
-    partners = peers + [x_device] + [z_device(s) for s in (1, -1, 2, -2)]
+    partners = peers + [sibling, x_device] + [z_device(s) for s in (1, -1, 2, -2)]
     for device in partners:
         pl.semaphore_signal(barrier, inc=1, device_id=device, device_id_type=MESH)
 
@@ -77,10 +73,10 @@
     for load in w_loads:
         load.start()
 
-    mine = pl.multiple_of(col * ROWS, ROWS)
+    chip = x_hi * 4 + y
 
     def send_all(slab, run, sem, recv):
-        block = seen.at[slab, run, pl.ds(mine, ROWS)]
+        block = seen.at[slab, run, chip, core]
         for device in peers:
             pltpu.make_async_remote_copy(
                 src_ref=block, dst_ref=block, send_sem=sem, recv_sem=recv,
@@ -90,11 +86,11 @@
     loads[0].wait()
     loads[1].wait()
     for run in range(RUNS):
-        seen[0, run, pl.ds(mine, ROWS), :] = older_v[pl.ds(run, ROWS, stride=2), :]
-        seen[1, run, pl.ds(mine, ROWS), :] = newer_v[pl.ds(run, ROWS, stride=2), :]
+        seen[0, run, chip, core] = older_v[pl.ds(run, ROWS, stride=2), :]
+        seen[1, run, chip, core] = newer_v[pl.ds(run, ROWS, stride=2), :]
     pl.semaphore_wait(barrier, len(partners))
     for run in range(RUNS):
-        for slab in range(2):
+        for slab in (1, 0):
             send_all(slab, run, first_send_sem.at[slab, run], gather_sem.at[slab, run])
 
     loads[2].wait()
@@ -120,9 +116,19 @@
 
     lax.fori_loop(0, 32, split, 0)
 
-    def gather_wait(slab, run):
-        rest = seen.at[slab, run, pl.ds(0, 15 * ROWS)]
-        pltpu.make_async_copy(rest, rest, gather_sem.at[slab, run]).wait()
+    def relay_copy(slab, run):
+        blocks = seen.at[slab, run, :, core]
+        sem = first_send_sem.at[slab, run] if slab < 2 else send_sem.at[slab - 2, run]
+        return pltpu.make_async_remote_copy(
+            src_ref=blocks, dst_ref=blocks, send_sem=sem, recv_sem=relay_sem.at[slab, run],
+            device_id=sibling, device_id_type=MESH,
+        )
+
+    def relay(slab, run):
+        for of in (1, 0) if slab == 0 else (slab + 1,):
+            rest = seen.at[of, run, pl.ds(0, 7), 0]
+            pltpu.make_async_copy(rest, rest, gather_sem.at[of, run]).wait()
+            relay_copy(of, run).start()
 
     def product(run, first, count):
         rows = pl.ds(first * ROWS, count * ROWS)
@@ -145,10 +151,12 @@
 
     def multiply(slab, run):
         if slab == 0:
-            gather_wait(0, run)
-        gather_wait(slab + 1, run)
+            relay_copy(0, run).wait_recv()
+        relay_copy(slab + 1, run).wait_recv()
         lag = jnp.broadcast_to(lag_class[0, 0], (16 * ROWS, LANES))
-        chosen = jnp.where(lag == 0, seen[slab + 1, run], seen[slab, run])
+        near = seen[slab + 1, run].reshape(16 * ROWS, LANES)
+        far = seen[slab, run].reshape(16 * ROWS, LANES)
+        chosen = jnp.where(lag == 0, near, far)
         high = chosen.astype(jnp.bfloat16)
         rhs[run, :, :LANES] = high
         rhs[run, :, LANES:] = (chosen - high.astype(jnp.float32)).astype(jnp.bfloat16)
@@ -165,59 +173,49 @@
         far, near = sign * (8 - 2 * step), sign * (7 - 2 * step)
         return (None if step == 0 and way != run else far), near
 
-    def z_copy(slab, run, way, step):
-        far, _ = pair_offsets(way, run, step)
-        first = 0 if far is not None else ROWS
-        rows = pl.ds(step * 2 * ROWS + first, 2 * ROWS - first)
+    def z_copy(slab, run, way, step, which, piece):
+        sign = 1 if way == 0 else -1
+        rows = pl.ds((step * 2 + which) * ROWS + piece * PIECE, PIECE)
+        at = ((step * 2 + which) * 2 + way) * PIECES + piece
         return pltpu.make_async_remote_copy(
             src_ref=z_send.at[slab, run, way, rows],
             dst_ref=z_recv.at[slab, run, way, rows],
             send_sem=send_sem.at[slab, run],
-            recv_sem=z_sem.at[slab, run, way, step],
-            device_id=z_device(2 if way == 0 else -2), device_id_type=MESH,
-        )
-
-    def last_copy(slab, run, way, which):
-        sign = 1 if way == 0 else -1
-        return pltpu.make_async_remote_copy(
-            src_ref=z_send.at[slab, run, way, pl.ds((6 + which) * ROWS, ROWS)],
-            dst_ref=z_last.at[slab, run, pl.ds((2 * way + which) * ROWS, ROWS)],
-            send_sem=send_sem.at[slab, run],
-            recv_sem=last_sem.at[slab, run, way, which],
-            device_id=z_device(sign * (2 - which)), device_id_type=MESH,
+            recv_sem=z_sem.at[slab, run, at],
+            device_id=z_device(sign * (1 if step == 3 and which == 1 else 2)),
+            device_id_type=MESH,
         )
 
     def pass_on(slab, run, step):
         x_copy(slab, run, step).wait_recv()
-        for way in range(2):
-            if step:
-                z_copy(slab, run, way, step - 1).wait_recv()
-            for which, offset in enumerate(pair_offsets(way, run, step)):
-                if offset is None:
-                    continue
-                at = PLACE[offset] * ROWS
-                total = (
-                    own[slab, run, at : at + ROWS, :] + x_recv[slab, run, at : at + ROWS, :]
-                )
-                if step and pair_offsets(way, run, step - 1)[which] is not None:
-                    came = ((step - 1) * 2 + which) * ROWS
-                    total = total + z_recv[slab, run, way, came : came + ROWS, :]
-                to = (step * 2 + which) * ROWS
-                z_send[slab, run, way, to : to + ROWS, :] = total
-            if step < 3:
-                z_copy(slab, run, way, step).start()
-            else:
-                for which in range(2):
-                    last_copy(slab, run, way, which).start()
+        for which in range(2):
+            for piece in range(PIECES):
+                for way in range(2):
+                    offset = pair_offsets(way, run, step)[which]
+                    if offset is None:
+                        continue
+                    at = PLACE[offset] * ROWS + piece * PIECE
+                    total = (
+                        own[slab, run, at : at + PIECE, :]
+                        + x_recv[slab, run, at : at + PIECE, :]
+                    )
+                    if step and pair_offsets(way, run, step - 1)[which] is not None:
+                        z_copy(slab, run, way, step - 1, which, piece).wait_recv()
+                        came = ((step - 1) * 2 + which) * ROWS + piece * PIECE
+                        total = total + z_recv[slab, run, way, came : came + PIECE, :]
+                    to = (step * 2 + which) * ROWS + piece * PIECE
+                    z_send[slab, run, way, to : to + PIECE, :] = total
+                    z_copy(slab, run, way, step, which, piece).start()
 
     def finish(slab, run):
         x_copy(slab, run, 4).wait_recv()
         total = own[slab, run, 15 * ROWS :, :] + x_recv[slab, run, 15 * ROWS :, :]
-        for which in (1, 0):
+        for which in range(2):
             for way in range(2):
-                last_copy(slab, run, way, which).wait_recv()
-                came = (2 * way + which) * ROWS
-                total = total + z_last[slab, run, came : came + ROWS, :]
+                for piece in range(PIECES):
+                    z_copy(slab, run, way, 3, which, piece).wait_recv()
+                came = (6 + which) * ROWS
+                total = total + z_recv[slab, run, way, came : came + ROWS, :]
         high = total.astype(jnp.bfloat16)
         low = (total - high.astype(jnp.float32)).astype(jnp.bfloat16)
         filtered = jnp.dot(high, kt_hi[...], preferred_element_type=jnp.float32) + (
@@ -227,7 +225,7 @@
         value = filtered + drive_v[slab, pl.ds(run, ROWS, stride=2), :]
         fresh = 1.0 / (1.0 + jnp.exp(-value))
         if slab < SLABS - 1:
-            seen[slab + 2, run, pl.ds(mine, ROWS), :] = fresh
+            seen[slab + 2, run, chip, core] = fresh
             send_all(slab + 2, run, send_sem.at[slab, run], gather_sem.at[slab + 2, run])
         out[slab, pl.ds(run, ROWS, stride=2), :] = fresh
 
@@ -235,6 +233,7 @@
     for run in range(RUNS):
         line = []
         for slab in range(SLABS):
+            line.append(functools.partial(relay, slab, run))
             line.append(functools.partial(multiply, slab, run))
             for step in range(4):
                 line.append(functools.partial(pass_on, slab, run, step))
@@ -247,8 +246,8 @@
 
     for run in range(RUNS):
         for slab in range(2):
-            rest = seen.at[slab, run, pl.ds(0, 15 * ROWS)]
-            pltpu.make_async_copy(rest, rest, first_send_sem.at[slab, run]).wait()
+            sent = w_raw.at[pl.ds(0, 15 * ROWS)]
+            pltpu.make_async_copy(sent, sent, first_send_sem.at[slab, run]).wait()
         for slab in range(SLABS):
             blocks = 16 + 15 + (15 if slab < SLABS - 1 else 0)
             sent = w_raw.at[pl.ds(0, blocks * ROWS)]
@@ -273,14 +272,13 @@
             pltpu.VMEM((4096, LANES), f32),
             pltpu.VMEM((1024, 512), bf16),
             pltpu.VMEM((1024, 512), bf16),
-            pltpu.VMEM((4, RUNS, 512, LANES), f32),
+            pltpu.VMEM((4, RUNS, 8, 2, ROWS, LANES), f32),
             pltpu.VMEM((RUNS, 512, 2 * LANES), bf16),
             pltpu.VMEM((SLABS, RUNS, 512, LANES), f32),
             pltpu.VMEM((SLABS, RUNS, 512, LANES), f32),
             pltpu.VMEM((SLABS, RUNS, 512, LANES), f32),
             pltpu.VMEM((SLABS, RUNS, 2, 8 * ROWS, LANES), f32),
             pltpu.VMEM((SLABS, RUNS, 2, 8 * ROWS, LANES), f32),
-            pltpu.VMEM((SLABS, RUNS, 4 * ROWS, LANES), f32),
             pltpu.VMEM((64, LANES), f32),
             pltpu.VMEM((64, LANES), f32),
             pltpu.VMEM((SLABS, 64, LANES), f32),
@@ -290,9 +288,9 @@
             pltpu.SemaphoreType.DMA((4,)),
             pltpu.SemaphoreType.DMA((32,)),
             pltpu.SemaphoreType.DMA((4, RUNS)),
+            pltpu.SemaphoreType.DMA((4, RUNS)),
             pltpu.SemaphoreType.DMA((SLABS, RUNS, 5)),
-            pltpu.SemaphoreType.DMA((SLABS, RUNS, 2, 3)),
-            pltpu.SemaphoreType.DMA((SLABS, RUNS, 2, 2)),
+            pltpu.SemaphoreType.DMA((SLABS, RUNS, 16 * PIECES)),
             pltpu.SemaphoreType.DMA((SLABS, RUNS)),
             pltpu.SemaphoreType.DMA((2, RUNS)),
         ],

time: 117 us -> 102 us (0.87)
  the two profiles are of different devices: /device:TPU:64 before, /device:TPU:2 now
where the time goes in v2:
time: 102 us
  Pallas kernels  99.5 us (98%)
  local copies, waits for them, and re-layouts  1.54 us (2%)
    pallas_call x1, Pallas kernels, per_device(): pl.pallas_call(kernel, out_shape=jax.ShapeDtypeStruct((SLABS, 64, LANES),...  99.5 us

profile of v2, /device:TPU:2, one launch (start us, length us, event | category | flops | bytes accessed | tf_op | source)
XLA Modules:
  0.0 101.7 jit_solution(13654466550211912773)
XLA Ops:
  0.7 99.5 %shard_map.64 = f32[3,64,128]{2,1,0:T(8,128)} custom-call(f32[4096,128]{1,0:T(8,128)} %bitcast.7, s32[1,1]{1,0:T(1,128)S(6)} %copy.9.lag_class, f32[64,128]{1,0:T(8,128)} %bitcast.10, f32[64,128]{1,0:T(8,128)} %bitcast.11, f32[3,64,128]{2,1,0:T(8,128)} %bitcast.9, f32[128,128]{1,0:T(8,128)} %syn_kernel.1), custom_call_target="tpu_custom_call" | custom-call | tf_op jit(solution)/shard_map/pallas_call | solution.py:259
  100.1 1.5 %copy.10 = f32[3,1,1,32,2,128]{5,4,3,2,1,0:T(2,128)} copy(f32[3,1,1,32,2,128]{5,4,3,2,1,0:T(2,128)} %bitcast.8) | data formatting | bytes 196608

commit v3 on v2

--- a/solution.py
+++ b/solution.py
@@ -13,8 +13,11 @@
 LANES = 128
 SLABS = 3
 RUNS = 2
-LAG = 1
+TAU = 4.0
+STAGE_US = (5.3, 6.5, 9.9, 12.6, 15.3, 18.0)
+SLAB_US = 19.5
 PIECE = 32
+AHEAD = 3
 
 OFFSETS = (8, 7, -7, 6, 5, -6, -5, 4, 3, -4, -3, 2, 1, -2, -1, 0)
 PLACE = {offset: place for place, offset in enumerate(OFFSETS)}
@@ -25,9 +28,9 @@
 
 def kernel(
     coupling, lag_class, older, newer, drive, syn_kernel, out,
-    w_raw, w_hi, w_lo, seen, rhs, own, x_send, x_recv, z_send, z_recv,
-    older_v, newer_v, drive_v, syn_v, kt_hi, kt_lo,
-    load_sem, w_sem, gather_sem, relay_sem, x_sem, z_sem, send_sem, first_send_sem,
+    w_raw, w_hi, w_lo, seen, rhs, own, x_send, x_recv, z_send, z_recv, d_recv,
+    older_v, newer_v, drive_v, syn_v, lag_v, kt_hi, kt_lo,
+    load_sem, w_sem, gather_sem, relay_sem, x_sem, z_sem, d_sem, send_sem, first_send_sem,
 ):
     row, col = lax.axis_index("row"), lax.axis_index("col")
     z, x_lo = row // 2, row % 2
@@ -36,14 +39,16 @@
     loads = [
         pltpu.make_async_copy(src, dst, load_sem.at[i])
         for i, (src, dst) in enumerate(
-            ((older, older_v), (newer, newer_v), (drive, drive_v), (syn_kernel, syn_v))
+            ((older, older_v), (newer, newer_v), (drive, drive_v), (syn_kernel, syn_v),
+             (lag_class, lag_v))
         )
     ]
     for load in loads:
         load.start()
 
-    def z_device(step):
-        return (lax.rem(z + step + N_Z, N_Z) * 2 + x_lo, col)
+    def z_device(step, across=False):
+        x_of = 1 - x_lo if across else x_lo
+        return (lax.rem(z + step + N_Z, N_Z) * 2 + x_of, col)
 
     x_device = (z * 2 + 1 - x_lo, col)
     peers = [
@@ -54,6 +59,7 @@
 
     barrier = pltpu.get_barrier_semaphore()
     partners = peers + [sibling, x_device] + [z_device(s) for s in (1, -1, 2, -2)]
+    partners += [z_device(2, True), z_device(-2, True)]
     for device in partners:
         pl.semaphore_signal(barrier, inc=1, device_id=device, device_id_type=MESH)
 
@@ -95,6 +101,7 @@
 
     loads[2].wait()
     loads[3].wait()
+    loads[4].wait()
     kt = syn_v[...].T
     kt_h = kt.astype(jnp.bfloat16)
     kt_hi[...] = kt_h
@@ -153,20 +160,34 @@
         if slab == 0:
             relay_copy(0, run).wait_recv()
         relay_copy(slab + 1, run).wait_recv()
-        lag = jnp.broadcast_to(lag_class[0, 0], (16 * ROWS, LANES))
+        lag = jnp.broadcast_to(lag_v[...], (16 * ROWS, LANES))
         near = seen[slab + 1, run].reshape(16 * ROWS, LANES)
         far = seen[slab, run].reshape(16 * ROWS, LANES)
         chosen = jnp.where(lag == 0, near, far)
         high = chosen.astype(jnp.bfloat16)
         rhs[run, :, :LANES] = high
         rhs[run, :, LANES:] = (chosen - high.astype(jnp.float32)).astype(jnp.bfloat16)
-        for group, (first, last) in enumerate(GROUPS):
-            x_send[slab, run, first * ROWS : last * ROWS, :] = product(run, first, last - first)
+        give(slab, run, 0)
+        keep(slab, run, 0)
+        pass_on(slab, run, 0)
+        for group in range(1, AHEAD):
+            give(slab, run, group)
+        keep(slab, run, 1)
+
+    def give(slab, run, group):
+        first, last = GROUPS[group]
+        x_send[slab, run, first * ROWS : last * ROWS, :] = product(run, first, last - first)
+        if group:
             x_copy(slab, run, group).start()
-        for first, last in GROUPS:
-            own[slab, run, first * ROWS : last * ROWS, :] = product(
-                run, 16 + first, last - first
-            )
+            return
+        for which in (0, 1):
+            for way in range(2):
+                if pair_offsets(way, run, 0)[which] is not None:
+                    d_copy(slab, run, way, which).start()
+
+    def keep(slab, run, group):
+        first, last = GROUPS[group]
+        own[slab, run, first * ROWS : last * ROWS, :] = product(run, 16 + first, last - first)
 
     def pair_offsets(way, run, step):
         sign = 1 if way == 0 else -1
@@ -186,8 +207,19 @@
             device_id_type=MESH,
         )
 
+    def d_copy(slab, run, way, which):
+        at = PLACE[pair_offsets(way, run, 0)[which]] * ROWS
+        return pltpu.make_async_remote_copy(
+            src_ref=x_send.at[slab, run, pl.ds(at, ROWS)],
+            dst_ref=d_recv.at[slab, run, pl.ds((way * 2 + which) * ROWS, ROWS)],
+            send_sem=send_sem.at[slab, run],
+            recv_sem=d_sem.at[slab, run, way * 2 + which],
+            device_id=z_device(2 if way == 0 else -2, True), device_id_type=MESH,
+        )
+
     def pass_on(slab, run, step):
-        x_copy(slab, run, step).wait_recv()
+        if step:
+            x_copy(slab, run, step).wait_recv()
         for which in range(2):
             for piece in range(PIECES):
                 for way in range(2):
@@ -195,17 +227,24 @@
                     if offset is None:
                         continue
                     at = PLACE[offset] * ROWS + piece * PIECE
-                    total = (
-                        own[slab, run, at : at + PIECE, :]
-                        + x_recv[slab, run, at : at + PIECE, :]
-                    )
+                    total = own[slab, run, at : at + PIECE, :]
+                    if step:
+                        total = total + x_recv[slab, run, at : at + PIECE, :]
                     if step and pair_offsets(way, run, step - 1)[which] is not None:
                         z_copy(slab, run, way, step - 1, which, piece).wait_recv()
                         came = ((step - 1) * 2 + which) * ROWS + piece * PIECE
                         total = total + z_recv[slab, run, way, came : came + PIECE, :]
+                        if step == 1:
+                            d_copy(slab, run, way, which).wait_recv()
+                            came = (way * 2 + which) * ROWS + piece * PIECE
+                            total = total + d_recv[slab, run, came : came + PIECE, :]
                     to = (step * 2 + which) * ROWS + piece * PIECE
                     z_send[slab, run, way, to : to + PIECE, :] = total
                     z_copy(slab, run, way, step, which, piece).start()
+        if step:
+            if step + AHEAD - 1 < 5:
+                give(slab, run, step + AHEAD - 1)
+            keep(slab, run, step + 1)
 
     def finish(slab, run):
         x_copy(slab, run, 4).wait_recv()
@@ -235,14 +274,17 @@
         for slab in range(SLABS):
             line.append(functools.partial(relay, slab, run))
             line.append(functools.partial(multiply, slab, run))
-            for step in range(4):
+            for step in range(1, 4):
                 line.append(functools.partial(pass_on, slab, run, step))
             line.append(functools.partial(finish, slab, run))
         stages.append(line)
-    for at in range(len(stages[0]) + LAG):
-        for run in range(RUNS):
-            if 0 <= at - LAG * run < len(stages[run]):
-                stages[run][at - LAG * run]()
+    order = []
+    for run in range(RUNS):
+        for at, stage in enumerate(stages[run]):
+            due = at // 6 * SLAB_US + STAGE_US[at % 6] + run * TAU
+            order.append((due, run, at, stage))
+    for _, _, _, stage in sorted(order, key=lambda entry: entry[:3]):
+        stage()
 
     for run in range(RUNS):
         for slab in range(2):
@@ -258,10 +300,10 @@
     f32, bf16 = jnp.float32, jnp.bfloat16
     rates = pl.pallas_call(
         kernel,
-        out_shape=jax.ShapeDtypeStruct((SLABS, 64, LANES), f32),
+        out_shape=pltpu.VMEM((SLABS, 64, LANES), f32),
         in_specs=[
             pl.BlockSpec(memory_space=pl.ANY),
-            pl.BlockSpec(memory_space=pltpu.SMEM),
+            pl.BlockSpec(memory_space=pl.ANY),
             pl.BlockSpec(memory_space=pl.ANY),
             pl.BlockSpec(memory_space=pl.ANY),
             pl.BlockSpec(memory_space=pl.ANY),
@@ -279,18 +321,21 @@
             pltpu.VMEM((SLABS, RUNS, 512, LANES), f32),
             pltpu.VMEM((SLABS, RUNS, 2, 8 * ROWS, LANES), f32),
             pltpu.VMEM((SLABS, RUNS, 2, 8 * ROWS, LANES), f32),
+            pltpu.VMEM((SLABS, RUNS, 4 * ROWS, LANES), f32),
             pltpu.VMEM((64, LANES), f32),
             pltpu.VMEM((64, LANES), f32),
             pltpu.VMEM((SLABS, 64, LANES), f32),
             pltpu.VMEM((LANES, LANES), f32),
+            pltpu.VMEM((1, 1), jnp.int32),
             pltpu.VMEM((LANES, LANES), bf16),
             pltpu.VMEM((LANES, LANES), bf16),
-            pltpu.SemaphoreType.DMA((4,)),
+            pltpu.SemaphoreType.DMA((5,)),
             pltpu.SemaphoreType.DMA((32,)),
             pltpu.SemaphoreType.DMA((4, RUNS)),
             pltpu.SemaphoreType.DMA((4, RUNS)),
             pltpu.SemaphoreType.DMA((SLABS, RUNS, 5)),
             pltpu.SemaphoreType.DMA((SLABS, RUNS, 16 * PIECES)),
+            pltpu.SemaphoreType.DMA((SLABS, RUNS, 4)),
             pltpu.SemaphoreType.DMA((SLABS, RUNS)),
             pltpu.SemaphoreType.DMA((2, RUNS)),
         ],

time: 102 us -> 96.6 us (0.947)
  Pallas kernels: 99.5 us -> 95.2 us
    pallas_call x1, Pallas kernels: 99.5 us -> 95.2 us  [per_device(): pl.pallas_call(kernel, out_shape=pltpu.VMEM((SLABS, 64, LANES), f32), in_...]
where the time goes in v3:
time: 96.6 us; the launch traced here: 96.5 us
  Pallas kernels  95.2 us (99%)
    pallas_call x1, Pallas kernels, per_device(): pl.pallas_call(kernel, out_shape=pltpu.VMEM((SLABS, 64, LANES), f32), in_...  95.2 us

profile of v3, /device:TPU:2, one launch (start us, length us, event | category | flops | bytes accessed | tf_op | source)
XLA Modules:
  0.0 96.5 jit_solution(11203464867337495797)
XLA Ops:
  0.7 95.2 %shard_map.64 = f32[3,64,128]{2,1,0:T(8,128)S(1)} custom-call(f32[4096,128]{1,0:T(8,128)} %bitcast.8, s32[1,1]{1,0:T(1,128)S(6)} %copy.10.lag_class, f32[64,128]{1,0:T(8,128)} %bitcast.10, f32[64,128]{1,0:T(8,128)} %bitcast.11, f32[3,64,128]{2,1,0:T(8,128)} %bitcast.9, f32[128,128]{1,0:T(8,128)} %syn_kernel.1), custom_call_target="tpu_custom_call" | custom-call | tf_op jit(solution)/shard_map/pallas_call | solution.py:301
  95.8 0.6 copy.9

commit v4 on v3

--- a/solution.py
+++ b/solution.py
@@ -13,7 +13,7 @@
 LANES = 128
 SLABS = 3
 RUNS = 2
-TAU = 4.0
+TAU = 3.0
 STAGE_US = (5.3, 6.5, 9.9, 12.6, 15.3, 18.0)
 SLAB_US = 19.5
 PIECE = 32
@@ -59,7 +59,7 @@
 
     barrier = pltpu.get_barrier_semaphore()
     partners = peers + [sibling, x_device] + [z_device(s) for s in (1, -1, 2, -2)]
-    partners += [z_device(2, True), z_device(-2, True)]
+    partners += [z_device(s, True) for s in (1, -1, 2, -2)]
     for device in partners:
         pl.semaphore_signal(barrier, inc=1, device_id=device, device_id_type=MESH)
 
@@ -203,7 +203,7 @@
             dst_ref=z_recv.at[slab, run, way, rows],
             send_sem=send_sem.at[slab, run],
             recv_sem=z_sem.at[slab, run, at],
-            device_id=z_device(sign * (1 if step == 3 and which == 1 else 2)),
+            device_id=z_device(sign * (2 - which)),
             device_id_type=MESH,
         )
 
@@ -214,13 +214,14 @@
             dst_ref=d_recv.at[slab, run, pl.ds((way * 2 + which) * ROWS, ROWS)],
             send_sem=send_sem.at[slab, run],
             recv_sem=d_sem.at[slab, run, way * 2 + which],
-            device_id=z_device(2 if way == 0 else -2, True), device_id_type=MESH,
+            device_id=z_device((2 - which) * (1 if way == 0 else -1), True),
+            device_id_type=MESH,
         )
 
     def pass_on(slab, run, step):
         if step:
             x_copy(slab, run, step).wait_recv()
-        for which in range(2):
+        for which in (1, 0) if step else (0, 1):
             for piece in range(PIECES):
                 for way in range(2):
                     offset = pair_offsets(way, run, step)[which]
@@ -230,14 +231,17 @@
                     total = own[slab, run, at : at + PIECE, :]
                     if step:
                         total = total + x_recv[slab, run, at : at + PIECE, :]
-                    if step and pair_offsets(way, run, step - 1)[which] is not None:
-                        z_copy(slab, run, way, step - 1, which, piece).wait_recv()
-                        came = ((step - 1) * 2 + which) * ROWS + piece * PIECE
-                        total = total + z_recv[slab, run, way, came : came + PIECE, :]
-                        if step == 1:
-                            d_copy(slab, run, way, which).wait_recv()
-                            came = (way * 2 + which) * ROWS + piece * PIECE
-                            total = total + d_recv[slab, run, came : came + PIECE, :]
+                    if step and which == 0:
+                        for past in range(2):
+                            if pair_offsets(way, run, step - 1)[past] is None:
+                                continue
+                            z_copy(slab, run, way, step - 1, past, piece).wait_recv()
+                            came = ((step - 1) * 2 + past) * ROWS + piece * PIECE
+                            total = total + z_recv[slab, run, way, came : came + PIECE, :]
+                            if step == 1:
+                                d_copy(slab, run, way, past).wait_recv()
+                                came = (way * 2 + past) * ROWS + piece * PIECE
+                                total = total + d_recv[slab, run, came : came + PIECE, :]
                     to = (step * 2 + which) * ROWS + piece * PIECE
                     z_send[slab, run, way, to : to + PIECE, :] = total
                     z_copy(slab, run, way, step, which, piece).start()

time: 96.6 us -> 92.7 us (0.960)
  Pallas kernels: 95.2 us -> 91.3 us
    pallas_call x1, Pallas kernels: 95.2 us -> 91.3 us  [per_device(): pl.pallas_call(kernel, out_shape=pltpu.VMEM((SLABS, 64, LANES), f32), in_...]
where the time goes in v4:
time: 92.7 us; the launch traced here: 92.6 us
  Pallas kernels  91.3 us (98%)
    pallas_call x1, Pallas kernels, per_device(): pl.pallas_call(kernel, out_shape=pltpu.VMEM((SLABS, 64, LANES), f32), in_...  91.3 us

profile of v4, /device:TPU:2, one launch (start us, length us, event | category | flops | bytes accessed | tf_op | source)
XLA Modules:
  0.0 92.6 jit_solution(6263718233340593525)
XLA Ops:
  0.7 91.3 %shard_map.64 = f32[3,64,128]{2,1,0:T(8,128)S(1)} custom-call(f32[4096,128]{1,0:T(8,128)} %bitcast.8, s32[1,1]{1,0:T(1,128)S(6)} %copy.10.lag_class, f32[64,128]{1,0:T(8,128)} %bitcast.10, f32[64,128]{1,0:T(8,128)} %bitcast.11, f32[3,64,128]{2,1,0:T(8,128)} %bitcast.9, f32[128,128]{1,0:T(8,128)} %syn_kernel.1), custom_call_target="tpu_custom_call" | custom-call | tf_op jit(solution)/shard_map/pallas_call | solution.py:305
  92.0 0.6 copy.9

commit v5 on v4

--- a/solution.py
+++ b/solution.py
@@ -136,12 +136,25 @@
             rest = seen.at[of, run, pl.ds(0, 7), 0]
             pltpu.make_async_copy(rest, rest, gather_sem.at[of, run]).wait()
             relay_copy(of, run).start()
+        prepare(slab, run, core)
+
+    def prepare(slab, run, of_core):
+        lag = jnp.broadcast_to(lag_v[...], (8 * ROWS, LANES)).reshape(8, ROWS, LANES)
+        chosen = jnp.where(
+            lag == 0, seen[slab + 1, run, :, of_core], seen[slab, run, :, of_core]
+        )
+        high = chosen.astype(jnp.bfloat16)
+        rhs[run, :, of_core, :, :LANES] = high
+        rhs[run, :, of_core, :, LANES:] = (
+            chosen - high.astype(jnp.float32)
+        ).astype(jnp.bfloat16)
 
     def product(run, first, count):
         rows = pl.ds(first * ROWS, count * ROWS)
-        both = jnp.dot(w_hi[rows, :], rhs[run], preferred_element_type=jnp.float32)
+        right = rhs[run].reshape(16 * ROWS, 2 * LANES)
+        both = jnp.dot(w_hi[rows, :], right, preferred_element_type=jnp.float32)
         low = jnp.dot(
-            w_lo[rows, :], rhs[run, :, :LANES], preferred_element_type=jnp.float32
+            w_lo[rows, :], right[:, :LANES], preferred_element_type=jnp.float32
         )
         return both[:, :LANES] + (both[:, LANES:] + low)
 
@@ -160,13 +173,7 @@
         if slab == 0:
             relay_copy(0, run).wait_recv()
         relay_copy(slab + 1, run).wait_recv()
-        lag = jnp.broadcast_to(lag_v[...], (16 * ROWS, LANES))
-        near = seen[slab + 1, run].reshape(16 * ROWS, LANES)
-        far = seen[slab, run].reshape(16 * ROWS, LANES)
-        chosen = jnp.where(lag == 0, near, far)
-        high = chosen.astype(jnp.bfloat16)
-        rhs[run, :, :LANES] = high
-        rhs[run, :, LANES:] = (chosen - high.astype(jnp.float32)).astype(jnp.bfloat16)
+        prepare(slab, run, 1 - core)
         give(slab, run, 0)
         keep(slab, run, 0)
         pass_on(slab, run, 0)
@@ -319,7 +326,7 @@
             pltpu.VMEM((1024, 512), bf16),
             pltpu.VMEM((1024, 512), bf16),
             pltpu.VMEM((4, RUNS, 8, 2, ROWS, LANES), f32),
-            pltpu.VMEM((RUNS, 512, 2 * LANES), bf16),
+            pltpu.VMEM((RUNS, 8, 2, ROWS, 2 * LANES), bf16),
             pltpu.VMEM((SLABS, RUNS, 512, LANES), f32),
             pltpu.VMEM((SLABS, RUNS, 512, LANES), f32),
             pltpu.VMEM((SLABS, RUNS, 512, LANES), f32),

time: 92.7 us -> 94.1 us (1.015)
  Pallas kernels: 91.3 us -> 92.6 us
    pallas_call x1, Pallas kernels: 91.3 us -> 92.6 us  [per_device(): pl.pallas_call(kernel, out_shape=pltpu.VMEM((SLABS, 64, LANES), f32), in_...]
where the time goes in v5:
time: 94.1 us; the launch traced here: 94 us
  Pallas kernels  92.6 us (98%)
    pallas_call x1, Pallas kernels, per_device(): pl.pallas_call(kernel, out_shape=pltpu.VMEM((SLABS, 64, LANES), f32), in_...  92.6 us

profile of v5, /device:TPU:2, one launch (start us, length us, event | category | flops | bytes accessed | tf_op | source)
XLA Modules:
  0.0 94.0 jit_solution(2120745414402859991)
XLA Ops:
  0.7 92.6 %shard_map.64 = f32[3,64,128]{2,1,0:T(8,128)S(1)} custom-call(f32[4096,128]{1,0:T(8,128)} %bitcast.8, s32[1,1]{1,0:T(1,128)S(6)} %copy.10.lag_class, f32[64,128]{1,0:T(8,128)} %bitcast.10, f32[64,128]{1,0:T(8,128)} %bitcast.11, f32[3,64,128]{2,1,0:T(8,128)} %bitcast.9, f32[128,128]{1,0:T(8,128)} %syn_kernel.1), custom_call_target="tpu_custom_call" | custom-call | tf_op jit(solution)/shard_map/pallas_call | solution.py:312
  93.3 0.6 copy.9
